TPU v7x, 32 devices: a whole 2x2x4 slice. The times are simulated.
32 devices in a mesh: groups: 2 (over y), seq: 4 (over z), rep: 2 (over x), fsdp: 2 (over core).
Axes of the slice: x: 2, y: 2, z: 4, core: 2. Of those that a mesh axis runs over, the one named last changes fastest.
Arguments:
- activations: bfloat16 [8, 512, 2048], P(('groups', 'rep', 'fsdp'), 'seq'), parts along dimension 0, may hold values from -6 to 6
- queries: bfloat16 [8, 512, 2048], P(('groups', 'rep', 'fsdp'), 'seq'), parts along dimension 0, may hold values from -102 to 102
- key_weight: bfloat16 [2048, 512], P(('seq', 'fsdp')), may hold values from -0.125 to 0.125
- value_weight: bfloat16 [2048, 512], P(('seq', 'fsdp')), may hold values from -0.125 to 0.125
- segment_ids: int32 [8, 512], P(('groups', 'rep', 'fsdp'), 'seq'), parts along dimension 0, may hold values from 0 to 3, never falling along the last dimension, each value on 1 to 384 neighbouring positions
- out_grad: bfloat16 [8, 512, 2048], P(('groups', 'rep', 'fsdp'), 'seq'), parts along dimension 0, may hold values from -6 to 6
Outputs:
- context: bfloat16 [8, 512, 2048], P(('groups', 'rep', 'fsdp'), 'seq'), parts along dimension 0
- query_grad: bfloat16 [8, 512, 2048], P(('groups', 'rep', 'fsdp'), 'seq'), parts along dimension 0
- input_grad: bfloat16 [8, 512, 2048], P(('groups', 'rep', 'fsdp'), 'seq'), parts along dimension 0
- key_weight_grad: bfloat16 [4096, 512], P(('groups', 'seq', 'fsdp')), parts along dimension 0
- value_weight_grad: bfloat16 [4096, 512], P(('groups', 'seq', 'fsdp')), parts along dimension 0
There are 2 independent parts, one for each index of `groups`. A program takes and returns all parts, laid end to end along the dimension named above; an argument that names none is the same for every part. Nothing has to cross between parts.
Inputs may be any that keep to these rules, and one draw needn't show every extreme that they name: `segment_ids`: document numbers never fall along a sequence; a document covers at most 384 positions.
All inputs are finite; a program needn't handle non-finite values.
Results may differ from a plain program's by a relative error of at most 0.025.
The roundings to bfloat16 on the way count: a program that leaves them out, or rounds other values in their place, can miss the bound.
Values may be sent and summed in bfloat16 or wider, within the bound.
No kernel may reach another device: no remote copies, remote signals or barrier semaphores. Data moves between devices by JAX's collectives and lax.ppermute only.
A program may use at most 64 MiB of HBM per device.

v0:
```python
import math
import jax
import jax.numpy as jnp
from jax import lax
from jax.sharding import PartitionSpec as P

HEADS = 16
KV_HEADS = 4
HEAD_DIM = 128
masked_low = -1e30


def block_mask(seg_all, row_start, col_start, block_width):
    row_pos = row_start + lax.iota(jnp.int32, block_width)
    col_pos = col_start + lax.iota(jnp.int32, block_width)
    seg_rows = lax.dynamic_slice_in_dim(seg_all, row_start, block_width)
    seg_cols = lax.dynamic_slice_in_dim(seg_all, col_start, block_width)
    return (col_pos[None, :] <= row_pos[:, None]) & (seg_cols[None, :] == seg_rows[:, None])


def block_scores(query_block, key_block, inv_root):
    return (
        jnp.einsum("qhd,khd->hqk", query_block, key_block, preferred_element_type=jnp.float32)
        * inv_root
    )


def take_block(source, index, block_width):
    return lax.dynamic_slice_in_dim(source, index * block_width, block_width, 0)


def attend(query_part, key_part, value_part, seg_all):
    length, heads_here, head_size = query_part.shape
    block_width = min(512, length)
    block_count = length // block_width
    inv_root = 1.0 / math.sqrt(head_size)

    def stats_row(i, log_totals):
        query_block = take_block(query_part, i, block_width)

        def stats_inner(j, state_now):
            running_max, running_sum = state_now
            scores = block_scores(query_block, take_block(key_part, j, block_width), inv_root)
            allowed = block_mask(seg_all, i * block_width, j * block_width, block_width)[None]
            scores = jnp.where(allowed, scores, masked_low)
            new_max = jnp.maximum(running_max, jnp.max(scores, axis=-1))
            weights = jnp.where(allowed, jnp.exp(scores - new_max[..., None]), 0.0)
            running_sum = running_sum * jnp.exp(running_max - new_max) + jnp.sum(weights, axis=-1)
            return (new_max, running_sum)

        start_state = (
            jnp.full((heads_here, block_width), masked_low, jnp.float32),
            jnp.zeros((heads_here, block_width), jnp.float32),
        )
        running_max, running_sum = lax.fori_loop(0, i + 1, stats_inner, start_state)
        return lax.dynamic_update_slice_in_dim(
            log_totals, running_max + jnp.log(running_sum), i * block_width, 1
        )

    log_totals = lax.fori_loop(
        0, block_count, stats_row, jnp.zeros((heads_here, length), jnp.float32)
    )

    def out_row(i, out_all):
        query_block = take_block(query_part, i, block_width)
        log_block = lax.dynamic_slice_in_dim(log_totals, i * block_width, block_width, 1)

        def out_inner(j, accum_out):
            scores = block_scores(query_block, take_block(key_part, j, block_width), inv_root)
            allowed = block_mask(seg_all, i * block_width, j * block_width, block_width)[None]
            probs_low = jnp.where(allowed, jnp.exp(scores - log_block[..., None]), 0.0).astype(
                jnp.bfloat16
            )
            return accum_out + jnp.einsum(
                "hqk,khd->qhd",
                probs_low,
                take_block(value_part, j, block_width),
                preferred_element_type=jnp.float32,
            )

        accum_out = lax.fori_loop(
            0, i + 1, out_inner, jnp.zeros((block_width, heads_here, head_size), jnp.float32)
        )
        return lax.dynamic_update_slice_in_dim(
            out_all, accum_out.astype(jnp.bfloat16), i * block_width, 0
        )

    out_all = lax.fori_loop(
        0, block_count, out_row, jnp.zeros((length, heads_here, head_size), jnp.bfloat16)
    )
    return (out_all, log_totals)


def attend_grads(query_part, key_part, value_part, seg_all, out_part, log_totals, grad_part):
    length, heads_here, head_size = query_part.shape
    block_width = min(512, length)
    block_count = length // block_width
    inv_root = 1.0 / math.sqrt(head_size)
    row_dots = jnp.einsum("qhd,qhd->hq", grad_part, out_part, preferred_element_type=jnp.float32)

    def grad_row(i, state_now):
        query_all, key_all, value_all = state_now
        query_block = take_block(query_part, i, block_width)
        grad_block = take_block(grad_part, i, block_width)
        log_block = lax.dynamic_slice_in_dim(log_totals, i * block_width, block_width, 1)
        dots_block = lax.dynamic_slice_in_dim(row_dots, i * block_width, block_width, 1)

        def grad_inner(j, inner_state):
            query_accum, key_accum, value_accum = inner_state
            key_block = take_block(key_part, j, block_width)
            value_block = take_block(value_part, j, block_width)
            scores = block_scores(query_block, key_block, inv_root)
            allowed = block_mask(seg_all, i * block_width, j * block_width, block_width)[None]
            probs = jnp.where(allowed, jnp.exp(scores - log_block[..., None]), 0.0)
            probs_low = probs.astype(jnp.bfloat16)
            value_new = take_block(value_accum, j, block_width) + jnp.einsum(
                "hqk,qhd->khd", probs_low, grad_block, preferred_element_type=jnp.float32
            )
            value_accum = lax.dynamic_update_slice_in_dim(
                value_accum, value_new, j * block_width, 0
            )
            prob_grad = jnp.einsum(
                "qhd,khd->hqk", grad_block, value_block, preferred_element_type=jnp.float32
            )
            score_grad = (probs * (prob_grad - dots_block[..., None])).astype(jnp.bfloat16)
            query_accum = query_accum + jnp.einsum(
                "hqk,khd->qhd", score_grad, key_block, preferred_element_type=jnp.float32
            )
            key_new = take_block(key_accum, j, block_width) + jnp.einsum(
                "hqk,qhd->khd", score_grad, query_block, preferred_element_type=jnp.float32
            )
            key_accum = lax.dynamic_update_slice_in_dim(key_accum, key_new, j * block_width, 0)
            return (query_accum, key_accum, value_accum)

        start_state = (
            jnp.zeros((block_width, heads_here, head_size), jnp.float32),
            key_all,
            value_all,
        )
        query_accum, key_all, value_all = lax.fori_loop(0, i + 1, grad_inner, start_state)
        query_all = lax.dynamic_update_slice_in_dim(
            query_all, (query_accum * inv_root).astype(jnp.bfloat16), i * block_width, 0
        )
        return (query_all, key_all, value_all)

    zero_grads = jnp.zeros((length, heads_here, head_size), jnp.float32)
    start_all = (jnp.zeros((length, heads_here, head_size), jnp.bfloat16), zero_grads, zero_grads)
    query_all, key_all, value_all = lax.fori_loop(0, block_count, grad_row, start_all)
    return (query_all, (key_all * inv_root).astype(jnp.bfloat16), value_all.astype(jnp.bfloat16))


def body(activations, queries, key_weight, value_weight, segment_ids, out_grad):
    rows_here = activations.shape[1]
    inputs = activations[0]
    kv_width = key_weight.shape[1]
    seq_devices = lax.axis_size("seq")
    heads_here = HEADS // seq_devices
    kv_group = HEADS // KV_HEADS
    stacked = jnp.concatenate([key_weight, value_weight], axis=1)
    columns = inputs
    projected = jnp.dot(
        columns,
        lax.all_gather(stacked, ("seq", "fsdp"), axis=0, tiled=True),
        preferred_element_type=jnp.float32,
    )
    projected = projected.astype(jnp.bfloat16)
    key_rows = projected[:, :kv_width].reshape(rows_here, KV_HEADS, HEAD_DIM)
    value_rows = projected[:, kv_width:].reshape(rows_here, KV_HEADS, HEAD_DIM)
    kv_copies = max(kv_group // heads_here, 1)
    query_heads = queries[0].reshape(rows_here, HEADS, HEAD_DIM)
    sent = (
        query_heads,
        jnp.repeat(key_rows, kv_copies, axis=1),
        jnp.repeat(value_rows, kv_copies, axis=1),
    )
    query_part, key_part, value_part = (
        lax.all_to_all(sent[0], "seq", split_axis=1, concat_axis=0, tiled=True),
        lax.all_to_all(sent[1], "seq", split_axis=1, concat_axis=0, tiled=True),
        lax.all_to_all(sent[2], "seq", split_axis=1, concat_axis=0, tiled=True),
    )
    widen_by = heads_here // key_part.shape[1]
    key_part = jnp.repeat(key_part, widen_by, axis=1)
    value_part = jnp.repeat(value_part, widen_by, axis=1)
    seg_all = lax.all_gather(segment_ids[0], "seq", axis=0, tiled=True)
    out_part, log_totals = attend(query_part, key_part, value_part, seg_all)
    context = lax.all_to_all(out_part, "seq", split_axis=0, concat_axis=1, tiled=True).reshape(
        1, rows_here, HEADS * HEAD_DIM
    )
    grad_part = lax.all_to_all(
        out_grad[0].reshape(rows_here, HEADS, HEAD_DIM),
        "seq",
        split_axis=1,
        concat_axis=0,
        tiled=True,
    )
    query_back, key_back, value_back = attend_grads(
        query_part, key_part, value_part, seg_all, out_part, log_totals, grad_part
    )
    query_tok, key_tok, value_tok = (
        lax.all_to_all(query_back, "seq", split_axis=0, concat_axis=1, tiled=True),
        lax.all_to_all(key_back, "seq", split_axis=0, concat_axis=1, tiled=True),
        lax.all_to_all(value_back, "seq", split_axis=0, concat_axis=1, tiled=True),
    )
    key_sum = (
        key_tok.reshape(rows_here, KV_HEADS, kv_group, HEAD_DIM).astype(jnp.float32).sum(axis=2)
    )
    value_sum = (
        value_tok.reshape(rows_here, KV_HEADS, kv_group, HEAD_DIM).astype(jnp.float32).sum(axis=2)
    )
    grad_kv = jnp.concatenate(
        [
            key_sum.astype(jnp.bfloat16).reshape(rows_here, kv_width),
            value_sum.astype(jnp.bfloat16).reshape(rows_here, kv_width),
        ],
        axis=1,
    )
    input_grad = lax.dot_general(
        grad_kv,
        lax.all_gather(stacked, ("seq", "fsdp"), axis=0, tiled=True),
        (((1,), (1,)), ((), ())),
        preferred_element_type=jnp.float32,
    )
    input_grad = input_grad.astype(jnp.bfloat16).reshape(1, rows_here, inputs.shape[1])
    columns = inputs
    grad_shard = lax.psum_scatter(
        lax.dot_general(
            columns, grad_kv, (((0,), (0,)), ((), ())), preferred_element_type=jnp.float32
        ).astype(jnp.bfloat16),
        ("seq", "fsdp"),
        scatter_dimension=0,
        tiled=True,
    ).astype(jnp.float32)
    grad_total = lax.psum(grad_shard, "rep").astype(jnp.bfloat16)
    query_grad = query_tok.reshape(1, rows_here, HEADS * HEAD_DIM)
    return (context, query_grad, input_grad, grad_total[:, :kv_width], grad_total[:, kv_width:])


def solution(mesh):
    return jax.shard_map(
        body,
        mesh=mesh,
        in_specs=(
            P(("groups", "rep", "fsdp"), "seq", None),
            P(("groups", "rep", "fsdp"), "seq", None),
            P(("seq", "fsdp"), None),
            P(("seq", "fsdp"), None),
            P(("groups", "rep", "fsdp"), "seq"),
            P(("groups", "rep", "fsdp"), "seq", None),
        ),
        out_specs=(
            P(("groups", "rep", "fsdp"), "seq", None),
            P(("groups", "rep", "fsdp"), "seq", None),
            P(("groups", "rep", "fsdp"), "seq", None),
            P(("groups", "seq", "fsdp"), None),
            P(("groups", "seq", "fsdp"), None),
        ),
        check_vma=False,
    )
```

profile of v0, /device:TPU:0, one launch (start us, length us, event | category | flops | bytes accessed | tf_op | source)
XLA Modules:
  0.0 248.5 jit_solution(1533762481953320926)
XLA Ops:
  7.2 0.0 copy-start
  7.2 0.0 all-gather.3.cloned.1.call-start
  7.2 1.9 pad_maximum_fusion
  9.2 0.0 all-gather.3.cloned.1.call-update
  9.2 2.0 copy.45
  11.2 6.3 %all-to-all-start.1 = ((bf16[128,16,128]{0,2,1:T(8,128)(2,1)}), bf16[128,16,128]{0,2,1:T(8,128)(2,1)S(1)}, u32[]{:S(2)}, u32[]{:S(2)}) async-start(bf16[128,16,128]{0,2,1:T(8,128)(2,1)} %bitcast.9), calls=%async_computation.1 | async-start | bytes 1048576 | tf_op jit(solution)/shard_map/all_to_all | solution.py:177
  17.5 2.0 copy.52
  19.6 24.7 %all-to-all-done.1 = bf16[128,16,128]{0,2,1:T(8,128)(2,1)S(1)} async-done(((bf16[128,16,128]{0,2,1:T(8,128)(2,1)}), bf16[128,16,128]{0,2,1:T(8,128)(2,1)S(1)}, u32[]{:S(2)}, u32[]{:S(2)}) %all-to-all-start.1) | async-done | bytes 524320 | tf_op jit(solution)/shard_map/all_to_all | solution.py:177
  44.2 3.6 %all-to-all-start.4 = ((bf16[128,16,128]{0,2,1:T(8,128)(2,1)}), bf16[128,16,128]{0,2,1:T(8,128)(2,1)S(1)}, u32[]{:S(2)}, u32[]{:S(2)}) async-start(bf16[128,16,128]{0,2,1:T(8,128)(2,1)} %bitcast.22), calls=%async_computation.4 | async-start | bytes 1048576 | tf_op jit(solution)/shard_map/all_to_all | solution.py:189
  47.9 0.0 copy-done.3
  47.9 21.7 %all-gather = s32[1,512]{1,0:T(1,128)S(1)} all-gather(s32[1,128]{1,0:T(1,128)S(1)} %copy-done.3), channel_id=2, replica_groups=mesh['groups'=2,'seq'=4,'rep'=2,'fsdp'=2] {'seq'}, dimensions={1}, use_global_device_ids=true | all-gather | bytes 2560 | tf_op jit(solution)/shard_map/all_gather | solution.py:184
  69.5 9.1 %all-gather.3.cloned.1.call-done = bf16[2048,1024]{1,0:T(8,128)(2,1)} async-done(((bf16[256,1024]{1,0:T(8,128)(2,1)}), bf16[2048,1024]{1,0:T(8,128)(2,1)}) %all-gather.3.cloned.1.call-update) | async-done | bytes 4194320 | tf_op jit(solution)/shard_map/all_gather | solution.py:163
  78.7 0.0 copy-done
  78.7 3.5 %fusion.11 = bf16[128,1024]{0,1:T(8,128)(2,1)S(1)} fusion(bf16[2048,1024]{1,0:T(8,128)(2,1)} %all-gather.3.cloned.1.call-done, bf16[1,128,2048]{2,1,0:T(8,128)(2,1)S(1)} %copy-done), kind=kOutput, calls=%fused_computation.22 | convolution fusion | flops 537001984 | bytes 4980736 | tf_op jit(solution)/shard_map/dot_general | solution.py:161
  82.2 0.8 copy.44
  83.0 0.0 all-to-all-done.4
  83.0 3.3 %all-to-all-start = ((bf16[128,4,128]{2,0,1:T(8,128)(2,1)}), bf16[128,4,128]{2,0,1:T(8,128)(2,1)S(1)}, u32[]{:S(2)}, u32[]{:S(2)}) async-start(bf16[128,4,128]{2,0,1:T(8,128)(2,1)} %copy.44), calls=%async_computation | async-start | bytes 262144 | tf_op jit(solution)/shard_map/all_to_all | solution.py:178
  86.3 0.2 fusion.13
  86.5 0.3 copy.47
  86.8 0.3 copy.54
  87.1 0.8 copy.48
  87.9 4.8 %all-to-all-done = bf16[128,4,128]{2,0,1:T(8,128)(2,1)S(1)} async-done(((bf16[128,4,128]{2,0,1:T(8,128)(2,1)}), bf16[128,4,128]{2,0,1:T(8,128)(2,1)S(1)}, u32[]{:S(2)}, u32[]{:S(2)}) %all-to-all-start) | async-done | bytes 131104 | tf_op jit(solution)/shard_map/all_to_all | solution.py:178
  92.7 3.3 %all-to-all-start.2 = ((bf16[128,4,128]{2,0,1:T(8,128)(2,1)}), bf16[128,4,128]{2,0,1:T(8,128)(2,1)S(1)}, u32[]{:S(2)}, u32[]{:S(2)}) async-start(bf16[128,4,128]{2,0,1:T(8,128)(2,1)} %copy.48), calls=%async_computation.2 | async-start | bytes 262144 | tf_op jit(solution)/shard_map/all_to_all | solution.py:179
  96.0 0.9 fusion.3
  96.9 0.0 copy-start.1
  96.9 1.0 select_reduce_fusion
  98.0 0.9 fusion.10
  99.0 0.0 copy-done.1
  99.0 1.2 copy.60
  100.2 1.8 all-to-all-done.2
  101.9 3.5 %all-to-all-start.7 = ((bf16[512,4,128]{2,1,0:T(4,128)(2,1)}), bf16[512,4,128]{2,1,0:T(4,128)(2,1)S(1)}, u32[]{:S(2)}, u32[]{:S(2)}) async-start(bf16[512,4,128]{2,1,0:T(4,128)(2,1)} %copy.60), calls=%async_computation.7 | async-start | bytes 1048576 | tf_op jit(solution)/shard_map/all_to_all | solution.py:202
  105.4 3.9 %fusion.12 = (f32[4,512]{1,0:T(4,128)S(1)}, bf16[4,512,128]{2,1,0:T(8,128)(2,1)S(1)}) fusion(bf16[4,128,4,128]{3,1,0,2:T(8,128)(2,1)S(1)} %copy.54, bf16[512,128]{1,0:T(8,128)(2,1)S(1)} %bitcast.111, f32[4,512,512]{2,1,0:T(8,128)} %copy-done.1, f32[4,512]{1,0:T(4,128)S(1)} %log_add_fusion, pred[512,512]{0,1:T(8,128)(4,1)S(1)} %fusion.13), kind=kOutput, calls=%fused_computation.24 | convolution fusion | flops 273938432 | bytes 5652480 | tf_op jit(solution)/shard_map/while/body/eval_jaxpr/while/body/hqk,khd->qhd/dot_general | solution.py:74
  109.3 1.4 fusion
  110.8 0.7 fusion.8
  111.5 0.6 copy-done.4
  112.1 1.2 copy.58
  113.3 5.2 %all-to-all-done.7 = bf16[512,4,128]{2,1,0:T(4,128)(2,1)S(1)} async-done(((bf16[512,4,128]{2,1,0:T(4,128)(2,1)}), bf16[512,4,128]{2,1,0:T(4,128)(2,1)S(1)}, u32[]{:S(2)}, u32[]{:S(2)}) %all-to-all-start.7) | async-done | bytes 524320 | tf_op jit(solution)/shard_map/all_to_all | solution.py:202
  118.5 3.5 %all-to-all-start.6 = ((bf16[512,4,128]{2,1,0:T(4,128)(2,1)}), bf16[512,4,128]{2,1,0:T(4,128)(2,1)S(1)}, u32[]{:S(2)}, u32[]{:S(2)}) async-start(bf16[512,4,128]{2,1,0:T(4,128)(2,1)} %copy.58), calls=%async_computation.6 | async-start | bytes 1048576 | tf_op jit(solution)/shard_map/all_to_all | solution.py:201
  122.0 0.2 reduce-scatter.2.cloned.1.call-start
  122.2 0.7 reduce_sum.48
  122.9 0.1 copy.61
  123.0 12.3 %all-to-all-done.6 = bf16[512,4,128]{2,1,0:T(4,128)(2,1)S(1)} async-done(((bf16[512,4,128]{2,1,0:T(4,128)(2,1)}), bf16[512,4,128]{2,1,0:T(4,128)(2,1)S(1)}, u32[]{:S(2)}, u32[]{:S(2)}) %all-to-all-start.6) | async-done | bytes 524320 | tf_op jit(solution)/shard_map/all_to_all | solution.py:201
  135.3 0.7 reduce_sum.45
  136.0 0.1 copy.59
  136.1 3.2 %convert_bitcast_fusion = bf16[2048,1024]{0,1:T(8,128)(2,1)} fusion(bf16[1,128,2048]{2,1,0:T(8,128)(2,1)S(1)} %copy-done, bf16[128,512]{0,1:T(8,128)(2,1)S(1)} %bitcast.98, bf16[128,512]{0,1:T(8,128)(2,1)S(1)} %bitcast.100), kind=kOutput, calls=%fused_computation.6 | convolution fusion | flops 539492352 | bytes 4980736 | tf_op jit(solution)/shard_map/dot_general | solution.py:226
  139.3 0.0 reduce-scatter.2.cloned.1.call-update
  139.4 1.2 copy.50
  140.6 3.5 %all-to-all-start.3 = ((bf16[512,4,128]{2,1,0:T(4,128)(2,1)}), bf16[512,4,128]{2,1,0:T(4,128)(2,1)S(1)}, u32[]{:S(2)}, u32[]{:S(2)}) async-start(bf16[512,4,128]{2,1,0:T(4,128)(2,1)} %copy.50), calls=%async_computation.3 | async-start | bytes 1048576 | tf_op jit(solution)/shard_map/all_to_all | solution.py:186
  144.1 0.9 fusion.9
  145.0 1.2 copy.56
  146.2 19.1 %all-to-all-done.3 = bf16[512,4,128]{2,1,0:T(4,128)(2,1)S(1)} async-done(((bf16[512,4,128]{2,1,0:T(4,128)(2,1)}), bf16[512,4,128]{2,1,0:T(4,128)(2,1)S(1)}, u32[]{:S(2)}, u32[]{:S(2)}) %all-to-all-start.3) | async-done | bytes 524320 | tf_op jit(solution)/shard_map/all_to_all | solution.py:186
  165.3 4.3 %all-to-all-start.5 = ((bf16[512,4,128]{2,1,0:T(4,128)(2,1)}), bf16[512,4,128]{2,1,0:T(4,128)(2,1)S(1)}, u32[]{:S(2)}, u32[]{:S(2)}) async-start(bf16[512,4,128]{2,1,0:T(4,128)(2,1)} %copy.56), calls=%async_computation.5 | async-start | bytes 1048576 | tf_op jit(solution)/shard_map/all_to_all | solution.py:200
  169.6 34.6 %reduce-scatter.2.cloned.1.call-done = bf16[256,1024]{0,1:T(8,128)(2,1)} async-done(((bf16[2048,1024]{0,1:T(8,128)(2,1)}), bf16[256,1024]{0,1:T(8,128)(2,1)}) %reduce-scatter.2.cloned.1.call-update) | async-done | bytes 524304 | tf_op jit(solution)/shard_map/reduce_scatter | solution.py:225
  204.2 0.0 all-reduce.2.cloned.1.call-update
  204.2 0.2 copy.51
  204.4 1.2 reshape.232
  205.6 0.0 all-to-all-done.5
  205.6 0.2 copy.57
  205.8 1.2 reshape.233
  207.0 4.5 %fusion.5 = bf16[1,128,2048]{2,1,0:T(8,128)(2,1)} fusion(bf16[2048,1024]{1,0:T(8,128)(2,1)} %all-gather.3.cloned.1.call-done, bf16[128,512]{0,1:T(8,128)(2,1)S(1)} %bitcast.99, bf16[128,512]{0,1:T(8,128)(2,1)S(1)} %bitcast.101), kind=kOutput, calls=%fused_computation.11 | convolution fusion | flops 537657344 | bytes 4980736 | tf_op jit(solution)/shard_map/dot_general | solution.py:217
  211.5 27.7 %all-reduce.2.cloned.1.call-done = bf16[256,1024]{0,1:T(8,128)(2,1)} async-done(((bf16[256,1024]{0,1:T(8,128)(2,1)}), bf16[256,1024]{0,1:T(8,128)(2,1)}) %all-reduce.2.cloned.1.call-update) | async-done | bytes 524304 | tf_op jit(solution)/shard_map/psum | solution.py:233
  239.2 1.1 fusion.25
  240.2 0.8 copy.63
  241.1 0.8 copy.62
  (10 shorter events, 0.1 us)
Async XLA Ops:
  7.2 71.5 %copy-start = (bf16[1,128,2048]{2,1,0:T(8,128)(2,1)S(1)}, bf16[1,128,2048]{2,1,0:T(8,128)(2,1)}, u32[]{:S(2)}) copy-start(bf16[1,128,2048]{2,1,0:T(8,128)(2,1)} %param.6) | copy-start | bytes 1572868
  7.2 40.7 %copy-start.3 = (s32[1,128]{1,0:T(1,128)S(1)}, s32[1,128]{1,0:T(1,128)}, u32[]{:S(2)}) copy-start(s32[1,128]{1,0:T(1,128)} %param.10) | copy-start | bytes 1540
  7.2 71.5 %all-gather.3.cloned.1.call-start = ((), (), s32[]{:S(2)}) async-start(), calls=%async_computation.9 | async-start | bytes 4718592 | tf_op jit(solution)/shard_map/all_gather | solution.py:163
  11.2 33.0 %all-to-all-start.1 = ((bf16[128,16,128]{0,2,1:T(8,128)(2,1)}), bf16[128,16,128]{0,2,1:T(8,128)(2,1)S(1)}, u32[]{:S(2)}, u32[]{:S(2)}) async-start(bf16[128,16,128]{0,2,1:T(8,128)(2,1)} %bitcast.9), calls=%async_computation.1 | async-start | bytes 1048576 | tf_op jit(solution)/shard_map/all_to_all | solution.py:177
  44.2 38.7 %all-to-all-start.4 = ((bf16[128,16,128]{0,2,1:T(8,128)(2,1)}), bf16[128,16,128]{0,2,1:T(8,128)(2,1)S(1)}, u32[]{:S(2)}, u32[]{:S(2)}) async-start(bf16[128,16,128]{0,2,1:T(8,128)(2,1)} %bitcast.22), calls=%async_computation.4 | async-start | bytes 1048576 | tf_op jit(solution)/shard_map/all_to_all | solution.py:189
  83.0 9.7 %all-to-all-start = ((bf16[128,4,128]{2,0,1:T(8,128)(2,1)}), bf16[128,4,128]{2,0,1:T(8,128)(2,1)S(1)}, u32[]{:S(2)}, u32[]{:S(2)}) async-start(bf16[128,4,128]{2,0,1:T(8,128)(2,1)} %copy.44), calls=%async_computation | async-start | bytes 262144 | tf_op jit(solution)/shard_map/all_to_all | solution.py:178
  92.7 9.2 %all-to-all-start.2 = ((bf16[128,4,128]{2,0,1:T(8,128)(2,1)}), bf16[128,4,128]{2,0,1:T(8,128)(2,1)S(1)}, u32[]{:S(2)}, u32[]{:S(2)}) async-start(bf16[128,4,128]{2,0,1:T(8,128)(2,1)} %copy.48), calls=%async_computation.2 | async-start | bytes 262144 | tf_op jit(solution)/shard_map/all_to_all | solution.py:179
  96.9 2.0 copy-start.1
  101.9 16.6 %all-to-all-start.7 = ((bf16[512,4,128]{2,1,0:T(4,128)(2,1)}), bf16[512,4,128]{2,1,0:T(4,128)(2,1)S(1)}, u32[]{:S(2)}, u32[]{:S(2)}) async-start(bf16[512,4,128]{2,1,0:T(4,128)(2,1)} %copy.60), calls=%async_computation.7 | async-start | bytes 1048576 | tf_op jit(solution)/shard_map/all_to_all | solution.py:202
  105.4 3.9 %copy-start.2 = (f32[4,512,512]{2,1,0:T(8,128)S(1)}, f32[4,512,512]{2,1,0:T(8,128)}, u32[]{:S(2)}) copy-start(f32[4,512,512]{2,1,0:T(8,128)} %copy-done.1) | copy-start | bytes 12582916
  110.7 1.4 copy-start.4
  118.5 16.8 %all-to-all-start.6 = ((bf16[512,4,128]{2,1,0:T(4,128)(2,1)}), bf16[512,4,128]{2,1,0:T(4,128)(2,1)S(1)}, u32[]{:S(2)}, u32[]{:S(2)}) async-start(bf16[512,4,128]{2,1,0:T(4,128)(2,1)} %copy.58), calls=%async_computation.6 | async-start | bytes 1048576 | tf_op jit(solution)/shard_map/all_to_all | solution.py:201
  122.0 82.2 %reduce-scatter.2.cloned.1.call-start = ((), (), s32[]{:S(2)}) async-start(), calls=%async_computation.10 | async-start | bytes 4718592 | tf_op jit(solution)/shard_map/reduce_scatter | solution.py:225
  139.3 4.7 %copy-start.5 = (bf16[4,512,512]{1,2,0:T(8,128)(2,1)S(1)}, bf16[4,512,512]{1,2,0:T(8,128)(2,1)}, u32[]{:S(2)}) copy-start(bf16[4,512,512]{1,2,0:T(8,128)(2,1)} %copy-done.4) | copy-start | bytes 6291460
  140.6 24.7 %all-to-all-start.3 = ((bf16[512,4,128]{2,1,0:T(4,128)(2,1)}), bf16[512,4,128]{2,1,0:T(4,128)(2,1)S(1)}, u32[]{:S(2)}, u32[]{:S(2)}) async-start(bf16[512,4,128]{2,1,0:T(4,128)(2,1)} %copy.50), calls=%async_computation.3 | async-start | bytes 1048576 | tf_op jit(solution)/shard_map/all_to_all | solution.py:186
  165.3 40.3 %all-to-all-start.5 = ((bf16[512,4,128]{2,1,0:T(4,128)(2,1)}), bf16[512,4,128]{2,1,0:T(4,128)(2,1)S(1)}, u32[]{:S(2)}, u32[]{:S(2)}) async-start(bf16[512,4,128]{2,1,0:T(4,128)(2,1)} %copy.56), calls=%async_computation.5 | async-start | bytes 1048576 | tf_op jit(solution)/shard_map/all_to_all | solution.py:200
  169.6 69.6 %all-reduce.2.cloned.1.call-start = ((), (), s32[]{:S(2)}) async-start(), calls=%async_computation.11 | async-start | bytes 1048576 | tf_op jit(solution)/shard_map/psum | solution.py:233
Sparse Core Ops, SparseCore 0:
  10.2 68.4 all-gather.2
  139.5 64.6 reduce-scatter.1
  206.5 32.6 all-reduce.1
where the time goes:
time: 249 us; the launch traced here: 248 us
  waiting for transfers between devices  139 us (56%)
  starting transfers between devices  31.6 us (13%)
  blocking collectives  21.7 us (9%)
  matrix products  19.9 us (8%)
  local copies, waits for them, and re-layouts  17.4 us (7%)
  between operations  14 us (6%)
  other arithmetic  4.52 us (2%)
    reduce_scatter x1, waiting for transfers between devices, body(): lax.psum_scatter(lax.dot_general(columns, grad_kv, (((0,), (0,)), ((), ()...  34.6 us
    psum x1, waiting for transfers between devices, body(): grad_total = lax.psum(grad_shard, 'rep').astype(jnp.bfloat16)  27.7 us
    all_to_all x1, waiting for transfers between devices, body(): lax.all_to_all(sent[0], 'seq', split_axis=1, concat_axis=0, tiled=True)  24.7 us
    all_gather x1, blocking collectives, body(): seg_all = lax.all_gather(segment_ids[0], 'seq', axis=0, tiled=True)  21.7 us
    all_to_all x1, waiting for transfers between devices, body(): lax.all_to_all(out_part, 'seq', split_axis=0, concat_axis=1, tiled=True)  19.1 us
    all_to_all x1, waiting for transfers between devices, body(): lax.all_to_all(key_back, 'seq', split_axis=0, concat_axis=1, tiled=True)  12.3 us
    all_gather x1, waiting for transfers between devices, body(): lax.all_gather(stacked, ('seq', 'fsdp'), axis=0, tiled=True)  9.14 us
    unnamed x16, local copies, waits for them, and re-layouts  6.44 us
  transfers between devices with their start and end apart: 11, of which 9 were waited for; matrix products, arithmetic and copies ran while one was open for 13% of the time, Pallas kernels for 0%

commit v1 on v0

--- a/solution.py
+++ b/solution.py
@@ -230,7 +230,13 @@
         scatter_dimension=0,
         tiled=True,
     ).astype(jnp.float32)
-    grad_total = lax.psum(grad_shard, "rep").astype(jnp.bfloat16)
+
+    def stocks_mark(local_array):
+        vec_out = lax.all_gather(local_array, axis_name="rep")
+        clean = jnp.sum(vec_out, 0)
+        return clean
+
+    grad_total = stocks_mark(grad_shard).astype(jnp.bfloat16)
     query_grad = query_tok.reshape(1, rows_here, HEADS * HEAD_DIM)
     return (context, query_grad, input_grad, grad_total[:, :kv_width], grad_total[:, kv_width:])
 

time: 249 us -> 246 us (0.988)
  waiting for transfers between devices: 139 us -> 128 us
  other arithmetic: 4.52 us -> 9.42 us
    psum x1 -> x0, waiting for transfers between devices: 27.7 us -> none  [body(): grad_total = lax.psum(grad_shard, 'rep').astype(jnp.bfloat16)]
    reduce_scatter x1, waiting for transfers between devices: 34.6 us -> 49.2 us  [body(): lax.psum_scatter(lax.dot_general(columns, grad_kv, (((0,), (0,)), ((), ()...]
    all_to_all x1, waiting for transfers between devices: 0.01 us -> 11.9 us  [body(): lax.all_to_all(query_back, 'seq', split_axis=0, concat_axis=1, tiled=True)]
    all_to_all x1, waiting for transfers between devices: 19.1 us -> 9.09 us  [body(): lax.all_to_all(out_part, 'seq', split_axis=0, concat_axis=1, tiled=True)]
    reduce_sum x0 -> x1, other arithmetic: none -> 2.78 us  [stocks_mark(): clean = jnp.sum(vec_out, 0)]
    all_gather x0 -> x1, local copies, waits for them, and re-layouts: none -> 2.56 us  [stocks_mark(): vec_out = lax.all_gather(local_array, axis_name='rep')]
    unnamed x16 -> x14, local copies, waits for them, and re-layouts: 6.44 us -> 6.43 us
  transfers between devices with their start and end apart: 11 -> 11, of which waited for: 9 -> 9; matrix products, arithmetic and copies ran while one was open for 13% -> 14% of each run, Pallas kernels for 0% -> 0%
where the time goes in v1:
time: 246 us; the launch traced here: 245 us
  waiting for transfers between devices  128 us (52%)
  starting transfers between devices  30.8 us (13%)
  matrix products  21.8 us (9%)
  blocking collectives  21.7 us (9%)
  local copies, waits for them, and re-layouts  18.9 us (8%)
  between operations  14 us (6%)
  other arithmetic  9.42 us (4%)
    reduce_scatter x1, waiting for transfers between devices, body(): lax.psum_scatter(lax.dot_general(columns, grad_kv, (((0,), (0,)), ((), ()...  49.2 us
    all_to_all x1, waiting for transfers between devices, body(): lax.all_to_all(sent[0], 'seq', split_axis=1, concat_axis=0, tiled=True)  24.7 us
    all_gather x1, blocking collectives, body(): seg_all = lax.all_gather(segment_ids[0], 'seq', axis=0, tiled=True)  21.7 us
    all_to_all x1, waiting for transfers between devices, body(): lax.all_to_all(key_back, 'seq', split_axis=0, concat_axis=1, tiled=True)  12.3 us
    all_to_all x1, waiting for transfers between devices, body(): lax.all_to_all(query_back, 'seq', split_axis=0, concat_axis=1, tiled=True)  11.9 us
    all_gather x1, waiting for transfers between devices, body(): lax.all_gather(stacked, ('seq', 'fsdp'), axis=0, tiled=True)  9.14 us
    all_to_all x1, waiting for transfers between devices, body(): lax.all_to_all(out_part, 'seq', split_axis=0, concat_axis=1, tiled=True)  9.09 us
    unnamed x14, local copies, waits for them, and re-layouts  6.43 us
  transfers between devices with their start and end apart: 11, of which 9 were waited for; matrix products, arithmetic and copies ran while one was open for 14% of the time, Pallas kernels for 0%

profile of v1, /device:TPU:0, one launch (start us, length us, event | category | flops | bytes accessed | tf_op | source)
XLA Modules:
  0.0 244.7 jit_solution(11198750569272864409)
XLA Ops:
  7.2 0.0 copy-start
  7.2 0.0 all-gather.5.cloned.1.call-start
  7.2 1.9 pad_maximum_fusion
  9.2 0.0 all-gather.5.cloned.1.call-update
  9.2 2.0 copy.39
  11.2 6.3 %all-to-all-start.1 = ((bf16[128,16,128]{0,2,1:T(8,128)(2,1)}), bf16[128,16,128]{0,2,1:T(8,128)(2,1)S(1)}, u32[]{:S(2)}, u32[]{:S(2)}) async-start(bf16[128,16,128]{0,2,1:T(8,128)(2,1)} %bitcast.9), calls=%async_computation.1 | async-start | bytes 1048576 | tf_op jit(solution)/shard_map/all_to_all | solution.py:177
  17.5 2.0 copy.46
  19.6 24.7 %all-to-all-done.1 = bf16[128,16,128]{0,2,1:T(8,128)(2,1)S(1)} async-done(((bf16[128,16,128]{0,2,1:T(8,128)(2,1)}), bf16[128,16,128]{0,2,1:T(8,128)(2,1)S(1)}, u32[]{:S(2)}, u32[]{:S(2)}) %all-to-all-start.1) | async-done | bytes 524320 | tf_op jit(solution)/shard_map/all_to_all | solution.py:177
  44.2 3.6 %all-to-all-start.4 = ((bf16[128,16,128]{0,2,1:T(8,128)(2,1)}), bf16[128,16,128]{0,2,1:T(8,128)(2,1)S(1)}, u32[]{:S(2)}, u32[]{:S(2)}) async-start(bf16[128,16,128]{0,2,1:T(8,128)(2,1)} %bitcast.22), calls=%async_computation.4 | async-start | bytes 1048576 | tf_op jit(solution)/shard_map/all_to_all | solution.py:189
  47.9 0.0 copy-done.3
  47.9 21.7 %all-gather = s32[1,512]{1,0:T(1,128)S(1)} all-gather(s32[1,128]{1,0:T(1,128)S(1)} %copy-done.3), channel_id=2, replica_groups=mesh['groups'=2,'seq'=4,'rep'=2,'fsdp'=2] {'seq'}, dimensions={1}, use_global_device_ids=true | all-gather | bytes 2560 | tf_op jit(solution)/shard_map/all_gather | solution.py:184
  69.5 9.1 %all-gather.5.cloned.1.call-done = bf16[2048,1024]{1,0:T(8,128)(2,1)} async-done(((bf16[256,1024]{1,0:T(8,128)(2,1)}), bf16[2048,1024]{1,0:T(8,128)(2,1)}) %all-gather.5.cloned.1.call-update) | async-done | bytes 4194320 | tf_op jit(solution)/shard_map/all_gather | solution.py:163
  78.7 0.0 copy-done
  78.7 3.5 %fusion.11 = bf16[128,1024]{0,1:T(8,128)(2,1)S(1)} fusion(bf16[2048,1024]{1,0:T(8,128)(2,1)} %all-gather.5.cloned.1.call-done, bf16[1,128,2048]{2,1,0:T(8,128)(2,1)S(1)} %copy-done), kind=kOutput, calls=%fused_computation.22 | convolution fusion | flops 537001984 | bytes 4980736 | tf_op jit(solution)/shard_map/dot_general | solution.py:161
  82.2 0.8 copy.38
  83.0 0.0 all-to-all-done.4
  83.0 3.3 %all-to-all-start = ((bf16[128,4,128]{2,0,1:T(8,128)(2,1)}), bf16[128,4,128]{2,0,1:T(8,128)(2,1)S(1)}, u32[]{:S(2)}, u32[]{:S(2)}) async-start(bf16[128,4,128]{2,0,1:T(8,128)(2,1)} %copy.38), calls=%async_computation | async-start | bytes 262144 | tf_op jit(solution)/shard_map/all_to_all | solution.py:178
  86.3 0.2 fusion.13
  86.5 0.3 copy.41
  86.8 0.3 copy.48
  87.1 0.8 copy.42
  87.9 4.8 %all-to-all-done = bf16[128,4,128]{2,0,1:T(8,128)(2,1)S(1)} async-done(((bf16[128,4,128]{2,0,1:T(8,128)(2,1)}), bf16[128,4,128]{2,0,1:T(8,128)(2,1)S(1)}, u32[]{:S(2)}, u32[]{:S(2)}) %all-to-all-start) | async-done | bytes 131104 | tf_op jit(solution)/shard_map/all_to_all | solution.py:178
  92.7 3.3 %all-to-all-start.2 = ((bf16[128,4,128]{2,0,1:T(8,128)(2,1)}), bf16[128,4,128]{2,0,1:T(8,128)(2,1)S(1)}, u32[]{:S(2)}, u32[]{:S(2)}) async-start(bf16[128,4,128]{2,0,1:T(8,128)(2,1)} %copy.42), calls=%async_computation.2 | async-start | bytes 262144 | tf_op jit(solution)/shard_map/all_to_all | solution.py:179
  96.0 0.9 fusion.3
  96.9 1.0 select_reduce_fusion
  98.0 0.9 fusion.10
  99.0 1.2 copy.54
  100.2 1.8 all-to-all-done.2
  101.9 3.5 %all-to-all-start.7 = ((bf16[512,4,128]{2,1,0:T(4,128)(2,1)}), bf16[512,4,128]{2,1,0:T(4,128)(2,1)S(1)}, u32[]{:S(2)}, u32[]{:S(2)}) async-start(bf16[512,4,128]{2,1,0:T(4,128)(2,1)} %copy.54), calls=%async_computation.7 | async-start | bytes 1048576 | tf_op jit(solution)/shard_map/all_to_all | solution.py:202
  105.4 3.9 %fusion.12 = (f32[4,512]{1,0:T(4,128)S(1)}, bf16[4,512,128]{2,1,0:T(8,128)(2,1)S(1)}) fusion(bf16[4,128,4,128]{3,1,0,2:T(8,128)(2,1)S(1)} %copy.48, bf16[512,128]{1,0:T(8,128)(2,1)S(1)} %bitcast.113, f32[4,512,512]{2,1,0:T(8,128)} %copy-done.1, f32[4,512]{1,0:T(4,128)S(1)} %log_add_fusion, pred[512,512]{0,1:T(8,128)(4,1)S(1)} %fusion.13), kind=kOutput, calls=%fused_computation.24 | convolution fusion | flops 273938432 | bytes 5652480 | tf_op jit(solution)/shard_map/while/body/eval_jaxpr/while/body/hqk,khd->qhd/dot_general | solution.py:74
  109.3 1.4 fusion
  110.8 0.7 fusion.8
  111.5 0.6 copy-done.4
  112.1 1.2 copy.52
  113.3 5.2 %all-to-all-done.7 = bf16[512,4,128]{2,1,0:T(4,128)(2,1)S(1)} async-done(((bf16[512,4,128]{2,1,0:T(4,128)(2,1)}), bf16[512,4,128]{2,1,0:T(4,128)(2,1)S(1)}, u32[]{:S(2)}, u32[]{:S(2)}) %all-to-all-start.7) | async-done | bytes 524320 | tf_op jit(solution)/shard_map/all_to_all | solution.py:202
  118.5 3.5 %all-to-all-start.6 = ((bf16[512,4,128]{2,1,0:T(4,128)(2,1)}), bf16[512,4,128]{2,1,0:T(4,128)(2,1)S(1)}, u32[]{:S(2)}, u32[]{:S(2)}) async-start(bf16[512,4,128]{2,1,0:T(4,128)(2,1)} %copy.52), calls=%async_computation.6 | async-start | bytes 1048576 | tf_op jit(solution)/shard_map/all_to_all | solution.py:201
  122.0 0.2 reduce-scatter.2.cloned.1.call-start
  122.2 0.7 reduce_sum.57
  122.9 0.1 copy.55
  123.0 12.3 %all-to-all-done.6 = bf16[512,4,128]{2,1,0:T(4,128)(2,1)S(1)} async-done(((bf16[512,4,128]{2,1,0:T(4,128)(2,1)}), bf16[512,4,128]{2,1,0:T(4,128)(2,1)S(1)}, u32[]{:S(2)}, u32[]{:S(2)}) %all-to-all-start.6) | async-done | bytes 524320 | tf_op jit(solution)/shard_map/all_to_all | solution.py:201
  135.3 0.7 reduce_sum.54
  136.0 0.1 copy.53
  136.1 3.2 %convert_bitcast_fusion = bf16[2048,1024]{0,1:T(8,128)(2,1)} fusion(bf16[1,128,2048]{2,1,0:T(8,128)(2,1)S(1)} %copy-done, bf16[128,512]{0,1:T(8,128)(2,1)S(1)} %bitcast.100, bf16[128,512]{0,1:T(8,128)(2,1)S(1)} %bitcast.102), kind=kOutput, calls=%fused_computation.6 | convolution fusion | flops 539492352 | bytes 4980736 | tf_op jit(solution)/shard_map/dot_general | solution.py:226
  139.3 0.0 reduce-scatter.2.cloned.1.call-update
  139.4 0.0 all-gather.7.cloned.1.call-start
  139.4 49.2 %reduce-scatter.2.cloned.1.call-done = bf16[256,1024]{0,1:T(8,128)(2,1)} async-done(((bf16[2048,1024]{0,1:T(8,128)(2,1)}), bf16[256,1024]{0,1:T(8,128)(2,1)}) %reduce-scatter.2.cloned.1.call-update) | async-done | bytes 524304 | tf_op jit(solution)/shard_map/reduce_scatter | solution.py:225
  188.6 2.1 all_gather.21
  190.7 0.0 all-gather.7.cloned.1.call-update
  190.7 1.2 copy.44
  191.9 3.5 %all-to-all-start.3 = ((bf16[512,4,128]{2,1,0:T(4,128)(2,1)}), bf16[512,4,128]{2,1,0:T(4,128)(2,1)S(1)}, u32[]{:S(2)}, u32[]{:S(2)}) async-start(bf16[512,4,128]{2,1,0:T(4,128)(2,1)} %copy.44), calls=%async_computation.3 | async-start | bytes 1048576 | tf_op jit(solution)/shard_map/all_to_all | solution.py:186
  195.4 2.7 %fusion.9 = bf16[512,4,128]{2,0,1:T(8,128)(2,1)S(1)} fusion(bf16[4,512,512]{1,2,0:T(8,128)(2,1)} %copy-done.4, bf16[512,128]{1,0:T(8,128)(2,1)S(1)} %bitcast.105), kind=kOutput, calls=%fused_computation.19 | convolution fusion | flops 268959744 | bytes 2752512 | tf_op jit(solution)/shard_map/while/body/eval_jaxpr/while/body/hqk,khd->qhd/dot_general | solution.py:126
  198.2 1.2 copy.50
  199.4 9.1 %all-to-all-done.3 = bf16[512,4,128]{2,1,0:T(4,128)(2,1)S(1)} async-done(((bf16[512,4,128]{2,1,0:T(4,128)(2,1)}), bf16[512,4,128]{2,1,0:T(4,128)(2,1)S(1)}, u32[]{:S(2)}, u32[]{:S(2)}) %all-to-all-start.3) | async-done | bytes 524320 | tf_op jit(solution)/shard_map/all_to_all | solution.py:186
  208.5 3.5 %all-to-all-start.5 = ((bf16[512,4,128]{2,1,0:T(4,128)(2,1)}), bf16[512,4,128]{2,1,0:T(4,128)(2,1)S(1)}, u32[]{:S(2)}, u32[]{:S(2)}) async-start(bf16[512,4,128]{2,1,0:T(4,128)(2,1)} %copy.50), calls=%async_computation.5 | async-start | bytes 1048576 | tf_op jit(solution)/shard_map/all_to_all | solution.py:200
  212.0 0.2 copy.45
  212.2 1.2 reshape.232
  213.3 11.9 %all-to-all-done.5 = bf16[512,4,128]{2,1,0:T(4,128)(2,1)S(1)} async-done(((bf16[512,4,128]{2,1,0:T(4,128)(2,1)}), bf16[512,4,128]{2,1,0:T(4,128)(2,1)S(1)}, u32[]{:S(2)}, u32[]{:S(2)}) %all-to-all-start.5) | async-done | bytes 524320 | tf_op jit(solution)/shard_map/all_to_all | solution.py:200
  225.2 0.2 copy.51
  225.4 1.2 reshape.233
  226.6 4.5 %fusion.5 = bf16[1,128,2048]{2,1,0:T(8,128)(2,1)} fusion(bf16[2048,1024]{1,0:T(8,128)(2,1)} %all-gather.5.cloned.1.call-done, bf16[128,512]{0,1:T(8,128)(2,1)S(1)} %bitcast.101, bf16[128,512]{0,1:T(8,128)(2,1)S(1)} %bitcast.103), kind=kOutput, calls=%fused_computation.11 | convolution fusion | flops 537657344 | bytes 4980736 | tf_op jit(solution)/shard_map/dot_general | solution.py:217
  231.1 2.6 %reshape.239 = f32[2,256,1024]{1,0,2:T(2,128)S(1)} reshape(f32[512,1024]{0,1:T(8,128)} %all-gather.7.cloned.1.call-done) | data formatting | bytes 4194304 | tf_op jit(solution)/shard_map/all_gather | solution.py:235
  233.6 2.8 %reduce_sum.60 = bf16[256,1024]{0,1:T(8,128)(2,1)S(1)} reduce(f32[2,256,1024]{1,0,2:T(2,128)S(1)} %reshape.239, f32[]{:T(128)} %constant.105.clone.1), dimensions={0}, to_apply=%region_5.6 | reduce | flops 262144 | bytes 2621444 | tf_op jit(solution)/shard_map/reduce_sum | solution.py:236
  236.5 0.8 copy.57
  237.3 0.8 copy.56
  (11 shorter events, 0.1 us)
Async XLA Ops:
  7.2 71.5 %copy-start = (bf16[1,128,2048]{2,1,0:T(8,128)(2,1)S(1)}, bf16[1,128,2048]{2,1,0:T(8,128)(2,1)}, u32[]{:S(2)}) copy-start(bf16[1,128,2048]{2,1,0:T(8,128)(2,1)} %param.6) | copy-start | bytes 1572868
  7.2 40.7 %copy-start.3 = (s32[1,128]{1,0:T(1,128)S(1)}, s32[1,128]{1,0:T(1,128)}, u32[]{:S(2)}) copy-start(s32[1,128]{1,0:T(1,128)} %param.10) | copy-start | bytes 1540
  7.2 71.5 %all-gather.5.cloned.1.call-start = ((), (), s32[]{:S(2)}) async-start(), calls=%async_computation.9 | async-start | bytes 4718592 | tf_op jit(solution)/shard_map/all_gather | solution.py:163
  11.2 33.0 %all-to-all-start.1 = ((bf16[128,16,128]{0,2,1:T(8,128)(2,1)}), bf16[128,16,128]{0,2,1:T(8,128)(2,1)S(1)}, u32[]{:S(2)}, u32[]{:S(2)}) async-start(bf16[128,16,128]{0,2,1:T(8,128)(2,1)} %bitcast.9), calls=%async_computation.1 | async-start | bytes 1048576 | tf_op jit(solution)/shard_map/all_to_all | solution.py:177
  44.2 38.7 %all-to-all-start.4 = ((bf16[128,16,128]{0,2,1:T(8,128)(2,1)}), bf16[128,16,128]{0,2,1:T(8,128)(2,1)S(1)}, u32[]{:S(2)}, u32[]{:S(2)}) async-start(bf16[128,16,128]{0,2,1:T(8,128)(2,1)} %bitcast.22), calls=%async_computation.4 | async-start | bytes 1048576 | tf_op jit(solution)/shard_map/all_to_all | solution.py:189
  83.0 9.7 %all-to-all-start = ((bf16[128,4,128]{2,0,1:T(8,128)(2,1)}), bf16[128,4,128]{2,0,1:T(8,128)(2,1)S(1)}, u32[]{:S(2)}, u32[]{:S(2)}) async-start(bf16[128,4,128]{2,0,1:T(8,128)(2,1)} %copy.38), calls=%async_computation | async-start | bytes 262144 | tf_op jit(solution)/shard_map/all_to_all | solution.py:178
  92.7 9.2 %all-to-all-start.2 = ((bf16[128,4,128]{2,0,1:T(8,128)(2,1)}), bf16[128,4,128]{2,0,1:T(8,128)(2,1)S(1)}, u32[]{:S(2)}, u32[]{:S(2)}) async-start(bf16[128,4,128]{2,0,1:T(8,128)(2,1)} %copy.42), calls=%async_computation.2 | async-start | bytes 262144 | tf_op jit(solution)/shard_map/all_to_all | solution.py:179
  96.9 2.0 copy-start.1
  101.9 16.6 %all-to-all-start.7 = ((bf16[512,4,128]{2,1,0:T(4,128)(2,1)}), bf16[512,4,128]{2,1,0:T(4,128)(2,1)S(1)}, u32[]{:S(2)}, u32[]{:S(2)}) async-start(bf16[512,4,128]{2,1,0:T(4,128)(2,1)} %copy.54), calls=%async_computation.7 | async-start | bytes 1048576 | tf_op jit(solution)/shard_map/all_to_all | solution.py:202
  105.4 3.9 %copy-start.2 = (f32[4,512,512]{2,1,0:T(8,128)S(1)}, f32[4,512,512]{2,1,0:T(8,128)}, u32[]{:S(2)}) copy-start(f32[4,512,512]{2,1,0:T(8,128)} %copy-done.1) | copy-start | bytes 12582916
  110.7 1.4 copy-start.4
  118.5 16.8 %all-to-all-start.6 = ((bf16[512,4,128]{2,1,0:T(4,128)(2,1)}), bf16[512,4,128]{2,1,0:T(4,128)(2,1)S(1)}, u32[]{:S(2)}, u32[]{:S(2)}) async-start(bf16[512,4,128]{2,1,0:T(4,128)(2,1)} %copy.52), calls=%async_computation.6 | async-start | bytes 1048576 | tf_op jit(solution)/shard_map/all_to_all | solution.py:201
  122.0 66.6 %reduce-scatter.2.cloned.1.call-start = ((), (), s32[]{:S(2)}) async-start(), calls=%async_computation.10 | async-start | bytes 4718592 | tf_op jit(solution)/shard_map/reduce_scatter | solution.py:225
  139.4 91.7 %all-gather.7.cloned.1.call-start = ((), (), s32[]{:S(2)}) async-start(), calls=%async_computation.11 | async-start | bytes 3145728 | tf_op jit(solution)/shard_map/all_gather | solution.py:235
  191.9 16.5 %all-to-all-start.3 = ((bf16[512,4,128]{2,1,0:T(4,128)(2,1)}), bf16[512,4,128]{2,1,0:T(4,128)(2,1)S(1)}, u32[]{:S(2)}, u32[]{:S(2)}) async-start(bf16[512,4,128]{2,1,0:T(4,128)(2,1)} %copy.44), calls=%async_computation.3 | async-start | bytes 1048576 | tf_op jit(solution)/shard_map/all_to_all | solution.py:186
  208.5 16.7 %all-to-all-start.5 = ((bf16[512,4,128]{2,1,0:T(4,128)(2,1)}), bf16[512,4,128]{2,1,0:T(4,128)(2,1)S(1)}, u32[]{:S(2)}, u32[]{:S(2)}) async-start(bf16[512,4,128]{2,1,0:T(4,128)(2,1)} %copy.50), calls=%async_computation.5 | async-start | bytes 1048576 | tf_op jit(solution)/shard_map/all_to_all | solution.py:200
Sparse Core Ops, SparseCore 0:
  10.2 68.4 all-gather.4
  139.5 49.0 reduce-scatter.1
  190.9 31.2 all-gather.6
